TPU v7x, 32 devices: a whole 2x2x4 slice. The times are simulated.
32 devices in a mesh: fsdp: 2 (over x), ctx: 4 (over z), tp: 4 (over y, core).
Axes of the slice: x: 2, y: 2, z: 4, core: 2. Of those that a mesh axis runs over, the one named last changes fastest.
Arguments:
- tokens: bfloat16 [4, 1024, 2048], P('fsdp', 'ctx'), may hold values from -36 to 36
- cotangent: bfloat16 [4, 1024, 2048], P('fsdp', 'ctx'), may hold values from -9 to 9
- lengths: int32 [4, 2], P('fsdp'), may hold values from 1 to 768, 1024 in all within a row
- deal: int32 [4, 1024], P('fsdp'), may hold values from 0 to 1023, each once within a row
- att_proj: float32 [3, 2048, 2048], P(None, ('fsdp', 'ctx'), 'tp'), may hold values from -0.125 to 0.125
- attn_out: float32 [2048, 2048], P(('fsdp', 'ctx'), 'tp'), may hold values from -0.75 to 0.75
- ff_proj: float32 [2, 2048, 8192], P(None, ('fsdp', 'ctx'), 'tp'), may hold values from -0.125 to 0.125
- ff_out: float32 [2048, 8192], P(('fsdp', 'ctx'), 'tp'), may hold values from -0.0625 to 0.0625
- att_proj_first: float32 [3, 2048, 2048], P(None, ('fsdp', 'ctx'), 'tp')
- attn_out_first: float32 [2048, 2048], P(('fsdp', 'ctx'), 'tp')
- ff_proj_first: float32 [2, 2048, 8192], P(None, ('fsdp', 'ctx'), 'tp')
- ff_out_first: float32 [2048, 8192], P(('fsdp', 'ctx'), 'tp')
- att_proj_second: float32 [3, 2048, 2048], P(None, ('fsdp', 'ctx'), 'tp'), as said below
- attn_out_second: float32 [2048, 2048], P(('fsdp', 'ctx'), 'tp'), as said below
- ff_proj_second: float32 [2, 2048, 8192], P(None, ('fsdp', 'ctx'), 'tp'), as said below
- ff_out_second: float32 [2048, 8192], P(('fsdp', 'ctx'), 'tp'), as said below
Outputs:
- block_out: bfloat16 [4, 1024, 2048], P('fsdp', 'ctx')
- input_grad: float32 [4, 1024, 2048], P('fsdp', 'ctx')
- grad_norm: float32 [1], replicated
- att_proj_grad: float32 [3, 2048, 2048], P(None, ('fsdp', 'ctx'), 'tp')
- attn_out_grad: float32 [2048, 2048], P(('fsdp', 'ctx'), 'tp')
- ff_proj_grad: float32 [2, 2048, 8192], P(None, ('fsdp', 'ctx'), 'tp')
- ff_out_grad: float32 [2048, 8192], P(('fsdp', 'ctx'), 'tp')
- att_proj_first_new: float32 [3, 2048, 2048], P(None, ('fsdp', 'ctx'), 'tp')
- attn_out_first_new: float32 [2048, 2048], P(('fsdp', 'ctx'), 'tp')
- ff_proj_first_new: float32 [2, 2048, 8192], P(None, ('fsdp', 'ctx'), 'tp')
- ff_out_first_new: float32 [2048, 8192], P(('fsdp', 'ctx'), 'tp')
- att_proj_second_new: float32 [3, 2048, 2048], P(None, ('fsdp', 'ctx'), 'tp')
- attn_out_second_new: float32 [2048, 2048], P(('fsdp', 'ctx'), 'tp')
- ff_proj_second_new: float32 [2, 2048, 8192], P(None, ('fsdp', 'ctx'), 'tp')
- ff_out_second_new: float32 [2048, 8192], P(('fsdp', 'ctx'), 'tp')
- att_proj_new: float32 [3, 2048, 2048], P(None, ('fsdp', 'ctx'), 'tp')
- attn_out_new: float32 [2048, 2048], P(('fsdp', 'ctx'), 'tp')
- ff_proj_new: float32 [2, 2048, 8192], P(None, ('fsdp', 'ctx'), 'tp')
- ff_out_new: float32 [2048, 8192], P(('fsdp', 'ctx'), 'tp')
- att_proj_low: bfloat16 [3, 2048, 2048], P(None, ('fsdp', 'ctx'), 'tp')
- attn_out_low: bfloat16 [2048, 2048], P(('fsdp', 'ctx'), 'tp')
- ff_proj_low: bfloat16 [2, 2048, 8192], P(None, ('fsdp', 'ctx'), 'tp')
- ff_out_low: bfloat16 [2048, 8192], P(('fsdp', 'ctx'), 'tp')
Inputs may be any that keep to these rules, and one draw needn't show every extreme that they name: `lengths`: each row sums to 1024 and no entry exceeds 768. `deal`: each row is a permutation of the positions of its pack. `att_proj_second`: every entry is positive. `attn_out_second`: every entry is positive. `ff_proj_second`: every entry is positive. `ff_out_second`: every entry is positive.
All inputs are finite; a program needn't handle non-finite values.
Results may differ from a plain program's by a relative error of at most 0.017.
Values may be sent and summed in bfloat16 or wider, within the bound.
A program may use at most 320 MiB of HBM per device.

v0:
```python
import jax
import jax.numpy as jnp
from jax import lax
from jax.sharding import PartitionSpec as P

D = 2048
HEAD_DIM = 128
STEP = 10
EPS_NORM = 1e-05
BETA_ONE = 0.9
BETA_TWO = 0.95
EPS_ADAM = 1e-08
DECAY = 0.1
MAX_NORM = 1.0
NEG_FILL = -1e30


def layer_norm(values):
    centre = values - jnp.mean(values, axis=-1, keepdims=True)
    spread = jnp.mean(centre * centre, axis=-1, keepdims=True)
    return centre * lax.rsqrt(spread + EPS_NORM)


def rotary(values, cos_table, sine_table):
    half_dim = values.shape[-1] // 2
    turned = jnp.concatenate([-values[..., half_dim:], values[..., :half_dim]], axis=-1)
    return values * cos_table + turned * sine_table


def rope_tables(places):
    freq_steps = jnp.arange(HEAD_DIM // 2, dtype=jnp.float32)
    inverse = jnp.power(10000.0, -2.0 * freq_steps / HEAD_DIM)
    angles = places.astype(jnp.float32)[:, None] * inverse[None, :]
    doubled = jnp.concatenate([angles, angles], axis=1)
    return (jnp.cos(doubled)[:, None, :], jnp.sin(doubled)[:, None, :])


def first_positions(deal_row, length_row):
    seq_ends = jnp.cumsum(length_row)
    starts = seq_ends - length_row
    inside = (deal_row[:, None] >= starts[None, :]) & (deal_row[:, None] < seq_ends[None, :])
    return jnp.sum(jnp.where(inside, starts[None, :], 0), axis=1)


def swiglu(gate_up):
    return gate_up[1] * jax.nn.sigmoid(gate_up[1]) * gate_up[0]


def adam_step(weight, grad_sum, first, second, clip_factor, learn_rate):
    clipped = grad_sum * clip_factor
    first_new = BETA_ONE * first + (1.0 - BETA_ONE) * clipped
    second_new = BETA_TWO * second + (1.0 - BETA_TWO) * clipped * clipped
    first_hat = first_new / (1.0 - BETA_ONE**STEP)
    second_hat = second_new / (1.0 - BETA_TWO**STEP)
    weight_new = weight - learn_rate * (
        first_hat / (jnp.sqrt(second_hat) + EPS_ADAM) + DECAY * weight
    )
    return (first_new, second_new, weight_new)


def tensor_sum(partial_sum):
    return lax.psum(partial_sum, "tp")


def gather_weights(att_proj, attn_out, ff_proj, ff_out):
    att_full, proj_full = (
        lax.all_gather(att_proj.astype(jnp.bfloat16), ("fsdp", "ctx"), axis=1, tiled=True),
        lax.all_gather(ff_proj.astype(jnp.bfloat16), ("fsdp", "ctx"), axis=1, tiled=True),
    )
    out_full, down_full = (
        lax.all_gather(attn_out.astype(jnp.bfloat16), ("fsdp", "ctx"), axis=0, tiled=True),
        lax.all_gather(ff_out.astype(jnp.bfloat16), ("fsdp", "ctx"), axis=0, tiled=True),
    )
    return (att_full, out_full, proj_full, down_full)


def reduce_grads(att_grad, out_grad, proj_grad, down_grad):
    att_part, proj_part = (
        lax.psum_scatter(
            att_grad.astype(jnp.bfloat16), ("fsdp", "ctx"), scatter_dimension=1, tiled=True
        ).astype(jnp.float32),
        lax.psum_scatter(
            proj_grad.astype(jnp.bfloat16), ("fsdp", "ctx"), scatter_dimension=1, tiled=True
        ).astype(jnp.float32),
    )
    out_part, down_part = (
        lax.psum_scatter(
            out_grad.astype(jnp.bfloat16), ("fsdp", "ctx"), scatter_dimension=0, tiled=True
        ).astype(jnp.float32),
        lax.psum_scatter(
            down_grad.astype(jnp.bfloat16), ("fsdp", "ctx"), scatter_dimension=0, tiled=True
        ).astype(jnp.float32),
    )
    return (att_part, out_part, proj_part, down_part)


def micro_step(resid_in, grad_out, deal_row, length_row, weights, ctx_index):
    att_full, out_full, proj_full, down_full = weights
    row_count = resid_in.shape[0]
    head_width = att_full.shape[2]
    local_heads = head_width // HEAD_DIM
    score_scale = HEAD_DIM ** (-0.5)
    key_first = first_positions(deal_row, length_row)
    query_place = lax.dynamic_slice_in_dim(deal_row, ctx_index * row_count, row_count)
    query_first = lax.dynamic_slice_in_dim(key_first, ctx_index * row_count, row_count)
    allowed = (deal_row[None, :] <= query_place[:, None]) & (
        deal_row[None, :] >= query_first[:, None]
    )
    cos_table, sine_table = rope_tables(query_place - query_first)
    normed_one, norm_one_pull = jax.vjp(layer_norm, resid_in)
    act_one = normed_one.astype(jnp.bfloat16)
    joint_qkv = jnp.einsum("td,cdf->ctf", act_one, att_full, preferred_element_type=jnp.float32)

    def turn_pair(query_raw, key_raw):
        return (rotary(query_raw, cos_table, sine_table), rotary(key_raw, cos_table, sine_table))

    (query_rot, key_rot), turn_pull = jax.vjp(
        turn_pair,
        joint_qkv[0].reshape(row_count, local_heads, HEAD_DIM),
        joint_qkv[1].reshape(row_count, local_heads, HEAD_DIM),
    )
    query_low = query_rot.astype(jnp.bfloat16)
    key_low = key_rot.reshape(row_count, head_width).astype(jnp.bfloat16)
    value_low = joint_qkv[2].astype(jnp.bfloat16)
    keys_flat, values_flat = (
        lax.all_gather(key_low, "ctx", axis=0, tiled=True),
        lax.all_gather(value_low, "ctx", axis=0, tiled=True),
    )
    pack_len = keys_flat.shape[0]
    keys_all = keys_flat.reshape(pack_len, local_heads, HEAD_DIM)
    values_all = values_flat.reshape(pack_len, local_heads, HEAD_DIM)

    def scores_of():
        raw_scores = (
            jnp.einsum("thd,khd->htk", query_low, keys_all, preferred_element_type=jnp.float32)
            * score_scale
        )
        return jnp.where(allowed[None], raw_scores, NEG_FILL)

    scores = scores_of()
    row_peak = jnp.max(scores, axis=2, keepdims=True)
    exp_scores = jnp.exp(scores - row_peak)
    row_mass = jnp.sum(exp_scores, axis=2, keepdims=True)
    log_mass = row_peak + jnp.log(row_mass)
    attended = jnp.einsum(
        "htk,khd->thd",
        (exp_scores / row_mass).astype(jnp.bfloat16),
        values_all,
        preferred_element_type=jnp.float32,
    )
    attended_low = attended.reshape(row_count, head_width).astype(jnp.bfloat16)
    attn_branch = tensor_sum(
        jnp.einsum("tf,df->td", attended_low, out_full, preferred_element_type=jnp.float32)
    )
    resid_mid = resid_in + attn_branch
    normed_two, norm_two_pull = jax.vjp(layer_norm, resid_mid)
    act_two = normed_two.astype(jnp.bfloat16)
    gate_up = jnp.einsum("td,cdf->ctf", act_two, proj_full, preferred_element_type=jnp.float32)
    hidden, glu_pull = jax.vjp(swiglu, gate_up)
    hidden_low = hidden.astype(jnp.bfloat16)
    ff_branch = tensor_sum(
        jnp.einsum("tf,df->td", hidden_low, down_full, preferred_element_type=jnp.float32)
    )
    block_rows = (resid_mid + ff_branch).astype(jnp.bfloat16)
    down_grad = jnp.einsum("td,tf->df", grad_out, hidden_low, preferred_element_type=jnp.float32)
    hidden_grad = jnp.einsum("td,df->tf", grad_out, down_full, preferred_element_type=jnp.float32)
    (gate_up_grad,) = glu_pull(hidden_grad)
    gate_up_low = gate_up_grad.astype(jnp.bfloat16)
    proj_grad = jnp.einsum("td,ctf->cdf", act_two, gate_up_low, preferred_element_type=jnp.float32)
    act_two_grad = tensor_sum(
        jnp.einsum("ctf,cdf->td", gate_up_low, proj_full, preferred_element_type=jnp.float32)
    )
    (mid_back,) = norm_two_pull(act_two_grad)
    mid_grad = mid_back + grad_out.astype(jnp.float32)
    mid_low = mid_grad.astype(jnp.bfloat16)
    out_grad = jnp.einsum("td,tf->df", mid_low, attended_low, preferred_element_type=jnp.float32)
    attended_grad = jnp.einsum("td,df->tf", mid_low, out_full, preferred_element_type=jnp.float32)
    attended_grad = attended_grad.astype(jnp.bfloat16).reshape(row_count, local_heads, HEAD_DIM)
    scores = scores_of()
    probs = jnp.exp(scores - log_mass)
    value_grad = jnp.einsum(
        "htk,thd->khd",
        probs.astype(jnp.bfloat16),
        attended_grad,
        preferred_element_type=jnp.float32,
    )
    prob_grad = jnp.einsum(
        "thd,khd->htk", attended_grad, values_all, preferred_element_type=jnp.float32
    )
    delta_rows = jnp.sum(probs * prob_grad, axis=2, keepdims=True)
    score_grad = (probs * (prob_grad - delta_rows)).astype(jnp.bfloat16)
    query_grad = (
        jnp.einsum("htk,khd->thd", score_grad, keys_all, preferred_element_type=jnp.float32)
        * score_scale
    )
    key_grad = (
        jnp.einsum("htk,thd->khd", score_grad, query_low, preferred_element_type=jnp.float32)
        * score_scale
    )
    key_mine, value_mine = (
        lax.psum_scatter(
            key_grad.reshape(pack_len, head_width), "ctx", scatter_dimension=0, tiled=True
        ),
        lax.psum_scatter(
            value_grad.reshape(pack_len, head_width), "ctx", scatter_dimension=0, tiled=True
        ),
    )
    query_raw_grad, key_raw_grad = turn_pull(
        (query_grad, key_mine.reshape(row_count, local_heads, HEAD_DIM))
    )
    joint_grad = jnp.stack(
        [
            query_raw_grad.reshape(row_count, head_width),
            key_raw_grad.reshape(row_count, head_width),
            value_mine,
        ]
    ).astype(jnp.bfloat16)
    att_grad = jnp.einsum("td,ctf->cdf", act_one, joint_grad, preferred_element_type=jnp.float32)
    act_one_grad = tensor_sum(
        jnp.einsum("ctf,cdf->td", joint_grad, att_full, preferred_element_type=jnp.float32)
    )
    (in_back,) = norm_one_pull(act_one_grad)
    input_grad = in_back + mid_grad
    return (block_rows, input_grad, (att_grad, out_grad, proj_grad, down_grad))


def shards(
    tokens,
    cotangent,
    lengths,
    deal,
    att_proj,
    attn_out,
    ff_proj,
    ff_out,
    att_proj_first,
    attn_out_first,
    ff_proj_first,
    ff_out_first,
    att_proj_second,
    attn_out_second,
    ff_proj_second,
    ff_out_second,
):
    ctx_index = lax.axis_index("ctx")
    micro_count = tokens.shape[0]
    block_list = []
    input_list = []
    totals = None
    for batch_slot in range(micro_count):
        weights = gather_weights(att_proj, attn_out, ff_proj, ff_out)
        block_rows, input_grad, local_grads = micro_step(
            tokens[batch_slot].astype(jnp.float32),
            cotangent[batch_slot],
            deal[batch_slot],
            lengths[batch_slot],
            weights,
            ctx_index,
        )
        block_list.append(block_rows)
        input_list.append(input_grad)
        step_grads = reduce_grads(local_grads[0], local_grads[1], local_grads[2], local_grads[3])
        if batch_slot == 0:
            totals = step_grads
        else:
            totals = jax.tree.map(jnp.add, totals, step_grads)
    att_total, out_total, proj_total, down_total = totals
    square_sums = lax.psum(
        (
            jnp.sum(att_total * att_total),
            jnp.sum(out_total * out_total),
            jnp.sum(proj_total * proj_total),
            jnp.sum(down_total * down_total),
        ),
        ("fsdp", "ctx", "tp"),
    )
    norm_value = jnp.sqrt(square_sums[0] + square_sums[1] + square_sums[2] + square_sums[3])
    clip_factor = jnp.minimum(1.0, MAX_NORM / (norm_value + 1e-06))
    base_rate = D ** (-0.5)
    out_rate = (D // 32) ** (-0.5)
    att_first_new, att_second_new, att_new = adam_step(
        att_proj, att_total, att_proj_first, att_proj_second, clip_factor, base_rate
    )
    out_first_new, out_second_new, out_new = adam_step(
        attn_out, out_total, attn_out_first, attn_out_second, clip_factor, out_rate
    )
    proj_first_new, proj_second_new, proj_new = adam_step(
        ff_proj, proj_total, ff_proj_first, ff_proj_second, clip_factor, base_rate
    )
    down_first_new, down_second_new, down_new = adam_step(
        ff_out, down_total, ff_out_first, ff_out_second, clip_factor, base_rate
    )
    return (
        jnp.stack(block_list),
        jnp.stack(input_list),
        norm_value.reshape(1),
        att_total,
        out_total,
        proj_total,
        down_total,
        att_first_new,
        out_first_new,
        proj_first_new,
        down_first_new,
        att_second_new,
        out_second_new,
        proj_second_new,
        down_second_new,
        att_new,
        out_new,
        proj_new,
        down_new,
        att_new.astype(jnp.bfloat16),
        out_new.astype(jnp.bfloat16),
        proj_new.astype(jnp.bfloat16),
        down_new.astype(jnp.bfloat16),
    )


def solution(mesh):
    in_specs = (
        P("fsdp", "ctx", None),
        P("fsdp", "ctx", None),
        P("fsdp", None),
        P("fsdp", None),
        P(None, ("fsdp", "ctx"), "tp"),
        P(("fsdp", "ctx"), "tp"),
        P(None, ("fsdp", "ctx"), "tp"),
        P(("fsdp", "ctx"), "tp"),
        P(None, ("fsdp", "ctx"), "tp"),
        P(("fsdp", "ctx"), "tp"),
        P(None, ("fsdp", "ctx"), "tp"),
        P(("fsdp", "ctx"), "tp"),
        P(None, ("fsdp", "ctx"), "tp"),
        P(("fsdp", "ctx"), "tp"),
        P(None, ("fsdp", "ctx"), "tp"),
        P(("fsdp", "ctx"), "tp"),
    )
    out_specs = (
        P("fsdp", "ctx", None),
        P("fsdp", "ctx", None),
        P(),
        P(None, ("fsdp", "ctx"), "tp"),
        P(("fsdp", "ctx"), "tp"),
        P(None, ("fsdp", "ctx"), "tp"),
        P(("fsdp", "ctx"), "tp"),
        P(None, ("fsdp", "ctx"), "tp"),
        P(("fsdp", "ctx"), "tp"),
        P(None, ("fsdp", "ctx"), "tp"),
        P(("fsdp", "ctx"), "tp"),
        P(None, ("fsdp", "ctx"), "tp"),
        P(("fsdp", "ctx"), "tp"),
        P(None, ("fsdp", "ctx"), "tp"),
        P(("fsdp", "ctx"), "tp"),
        P(None, ("fsdp", "ctx"), "tp"),
        P(("fsdp", "ctx"), "tp"),
        P(None, ("fsdp", "ctx"), "tp"),
        P(("fsdp", "ctx"), "tp"),
        P(None, ("fsdp", "ctx"), "tp"),
        P(("fsdp", "ctx"), "tp"),
        P(None, ("fsdp", "ctx"), "tp"),
        P(("fsdp", "ctx"), "tp"),
    )
    return jax.shard_map(shards, mesh=mesh, in_specs=in_specs, out_specs=out_specs, check_vma=False)
```

profile of v0, /device:TPU:0, one launch (start us, length us, event | category | flops | bytes accessed | tf_op | source)
XLA Modules:
  0.0 2617.0 jit_solution(11051854917980619340)
XLA Ops:
  14.9 97.6 %all-gather.11.cloned.1.call-done = bf16[3,2048,512]{2,1,0:T(8,128)(2,1)} async-done(((bf16[3,256,512]{2,1,0:T(8,128)(2,1)}), bf16[3,2048,512]{2,1,0:T(8,128)(2,1)}) %all-gather.11.cloned.1.call-update) | async-done | bytes 6291472 | tf_op jit(solution)/shard_map/all_gather | solution.py:67
  112.5 4.6 convolution_bitcast_fusion.6
  132.8 4.8 convolution_bitcast_fusion.7
  148.3 5.8 all-gather.21.cloned.1.call-done
  155.6 28.1 %all-gather.25.cloned.1.call-done = bf16[1,1024,512]{2,1,0:T(8,128)(2,1)} async-done(((bf16[1,256,512]{2,1,0:T(8,128)(2,1)}), bf16[1,1024,512]{2,1,0:T(8,128)(2,1)}) %all-gather.25.cloned.1.call-update) | async-done | bytes 1048592 | tf_op jit(solution)/shard_map/all_gather | solution.py:127
  185.1 28.1 %all-gather.13.cloned.1.call-done = bf16[1024,512]{1,0:T(8,128)(2,1)} async-done(((bf16[256,512]{1,0:T(8,128)(2,1)}), bf16[1024,512]{1,0:T(8,128)(2,1)}) %all-gather.13.cloned.1.call-update) | async-done | bytes 1048592 | tf_op jit(solution)/shard_map/all_gather | solution.py:126
  214.7 27.9 %all-gather.23.cloned.1.call-done = bf16[1,1024,512]{2,1,0:T(8,128)(2,1)} async-done(((bf16[1,256,512]{2,1,0:T(8,128)(2,1)}), bf16[1,1024,512]{2,1,0:T(8,128)(2,1)}) %all-gather.23.cloned.1.call-update) | async-done | bytes 1048592 | tf_op jit(solution)/shard_map/all_gather | solution.py:127
  253.3 40.7 %all-gather.15.cloned.1.call-done = bf16[2048,512]{1,0:T(8,128)(2,1)} async-done(((bf16[256,512]{1,0:T(8,128)(2,1)}), bf16[2048,512]{1,0:T(8,128)(2,1)}) %all-gather.15.cloned.1.call-update) | async-done | bytes 2097168 | tf_op jit(solution)/shard_map/all_gather | solution.py:71
  294.0 3.8 fusion.144
  300.0 3.8 convert_element_type.242
  307.0 77.2 %all-reduce.25.cloned.1.call-done = (f32[256,2048]{1,0:T(8,128)}, f32[256,2048]{1,0:T(8,128)}) async-done(((f32[256,2048]{1,0:T(8,128)}, f32[256,2048]{1,0:T(8,128)}), (f32[256,2048]{1,0:T(8,128)}, f32[256,2048]{1,0:T(8,128)})) %all-reduce.25.cloned.1.call-update) | async-done | bytes 4194320 | tf_op jit(solution)/shard_map/psum | solution.py:62
  384.3 3.4 fusion.126
  389.5 225.4 %all-gather.17.cloned.1.call-done = bf16[2,2048,2048]{2,1,0:T(8,128)(2,1)} async-done(((bf16[2,256,2048]{2,1,0:T(8,128)(2,1)}), bf16[2,2048,2048]{2,1,0:T(8,128)(2,1)}) %all-gather.17.cloned.1.call-update) | async-done | bytes 16777232 | tf_op jit(solution)/shard_map/all_gather | solution.py:68
  615.0 13.2 convolution_bitcast_fusion
  628.1 6.3 convolution_bitcast_fusion.1
  634.4 106.6 %all-gather.19.cloned.1.call-done = bf16[2048,2048]{1,0:T(8,128)(2,1)} async-done(((bf16[256,2048]{1,0:T(8,128)(2,1)}), bf16[2048,2048]{1,0:T(8,128)(2,1)}) %all-gather.19.cloned.1.call-update) | async-done | bytes 8388624 | tf_op jit(solution)/shard_map/all_gather | solution.py:72
  741.0 10.6 multiply_bitcast_fusion.1
  751.6 5.9 multiply_bitcast_fusion.3
  757.5 13.5 convolution_bitcast_fusion.4
  771.0 13.9 convolution_bitcast_fusion.5
  785.7 83.3 %all-reduce.23.cloned.1.call-done = (f32[256,2048]{1,0:T(8,128)}, f32[256,2048]{1,0:T(8,128)}) async-done(((f32[256,2048]{1,0:T(8,128)}, f32[256,2048]{1,0:T(8,128)}), (f32[256,2048]{1,0:T(8,128)}, f32[256,2048]{1,0:T(8,128)})) %all-reduce.23.cloned.1.call-update) | async-done | bytes 4194320 | tf_op jit(solution)/shard_map/psum | solution.py:62
  881.9 4.1 multiply_reduce_fusion.2
  889.8 3.3 convolution_convert_fusion.2
  894.9 4.2 multiply_reduce_fusion.1
  903.1 4.4 fusion.30
  911.4 4.4 fusion.28
  919.7 3.3 convolution_convert_fusion
  923.0 8.5 fusion.55
  931.6 7.3 fusion.53
  941.1 3.7 broadcast_multiply_fusion.1
  953.4 25.2 reduce-scatter.17.cloned.1.call-done
  980.1 44.6 %reduce-scatter.15.cloned.1.call-done = f32[256,512]{1,0:T(8,128)} async-done(((f32[1024,512]{1,0:T(8,128)}), f32[256,512]{1,0:T(8,128)}) %reduce-scatter.15.cloned.1.call-update) | async-done | bytes 524304 | tf_op jit(solution)/shard_map/reduce_scatter | solution.py:204
  1025.8 45.0 %reduce-scatter.19.cloned.1.call-done = f32[256,512]{1,0:T(8,128)} async-done(((f32[1024,512]{1,0:T(8,128)}), f32[256,512]{1,0:T(8,128)}) %reduce-scatter.19.cloned.1.call-update) | async-done | bytes 524304 | tf_op jit(solution)/shard_map/reduce_scatter | solution.py:204
  1071.8 6.0 convolution_bitcast_fusion.3
  1077.8 6.0 convolution_bitcast_fusion.2
  1084.3 8.3 convert_bitcast_fusion.2
  1092.7 8.5 convert_bitcast_fusion.3
  1101.8 5.8 convert_bitcast_fusion.4
  1108.6 5.9 convert_bitcast_fusion.5
  1115.1 14.1 convert_bitcast_fusion
  1129.8 11.3 convert_bitcast_fusion.1
  1144.2 5.3 copy.151
  1158.6 5.4 copy.146
  1164.0 5.4 copy.143
  1175.2 36.4 %reduce-scatter.25.cloned.1.call-done = bf16[256,512]{1,0:T(8,128)(2,1)} async-done(((bf16[2048,512]{1,0:T(8,128)(2,1)}), bf16[256,512]{1,0:T(8,128)(2,1)}) %reduce-scatter.25.cloned.1.call-update) | async-done | bytes 262160 | tf_op jit(solution)/shard_map/reduce_scatter | solution.py:87
  1214.1 154.7 %all-reduce.21.cloned.1.call-done = (f32[256,2048]{1,0:T(8,128)}, f32[256,2048]{1,0:T(8,128)}, f32[256,2048]{1,0:T(8,128)}, f32[256,2048]{1,0:T(8,128)}) async-done(((f32[256,2048]{1,0:T(8,128)}, f32[256,2048]{1,0:T(8,128)}, f32[256,2048]{1,0:T(8,128)}, f32[256,2048]{1,0:T(8,128)}), (f32[256,2048]{1,0:T(8,128)}, f32[256,2048]{1,0:T(8,128)}, f32[256,2048]{1,0:T(8,128)}, ...) | async-done | bytes 8388624 | tf_op jit(solution)/shard_map/psum | solution.py:62
  1368.8 3.7 fusion.19
  1385.3 136.6 %reduce-scatter.35.cloned.1.call-done = bf16[256,2048]{0,1:T(8,128)(2,1)} async-done(((bf16[2048,2048]{0,1:T(8,128)(2,1)}), bf16[256,2048]{0,1:T(8,128)(2,1)}) %reduce-scatter.35.cloned.1.call-update) | async-done | bytes 1048592 | tf_op jit(solution)/shard_map/reduce_scatter | solution.py:90
  1521.9 152.5 %reduce-scatter.33.cloned.1.call-done = bf16[256,2048]{0,1:T(8,128)(2,1)} async-done(((bf16[2048,2048]{0,1:T(8,128)(2,1)}), bf16[256,2048]{0,1:T(8,128)(2,1)}) %reduce-scatter.33.cloned.1.call-update) | async-done | bytes 1048592 | tf_op jit(solution)/shard_map/reduce_scatter | solution.py:90
  1677.1 118.2 %reduce-scatter.23.cloned.1.call-done = bf16[3,256,512]{1,2,0:T(8,128)(2,1)} async-done(((bf16[3,2048,512]{1,2,0:T(8,128)(2,1)}), bf16[3,256,512]{1,2,0:T(8,128)(2,1)}) %reduce-scatter.23.cloned.1.call-update) | async-done | bytes 786448 | tf_op jit(solution)/shard_map/reduce_scatter | solution.py:79
  1795.2 121.2 %reduce-scatter.21.cloned.1.call-done = bf16[3,256,512]{1,2,0:T(8,128)(2,1)} async-done(((bf16[3,2048,512]{1,2,0:T(8,128)(2,1)}), bf16[3,256,512]{1,2,0:T(8,128)(2,1)}) %reduce-scatter.21.cloned.1.call-update) | async-done | bytes 786448 | tf_op jit(solution)/shard_map/reduce_scatter | solution.py:79
  1920.1 281.2 %reduce-scatter.31.cloned.1.call-done = bf16[2,256,2048]{1,2,0:T(8,128)(2,1)} async-done(((bf16[2,2048,2048]{1,2,0:T(8,128)(2,1)}), bf16[2,256,2048]{1,2,0:T(8,128)(2,1)}) %reduce-scatter.31.cloned.1.call-update) | async-done | bytes 2097168 | tf_op jit(solution)/shard_map/reduce_scatter | solution.py:82
  2201.4 285.4 %reduce-scatter.29.cloned.1.call-done = bf16[2,256,2048]{1,2,0:T(8,128)(2,1)} async-done(((bf16[2,2048,2048]{1,2,0:T(8,128)(2,1)}), bf16[2,256,2048]{1,2,0:T(8,128)(2,1)}) %reduce-scatter.29.cloned.1.call-update) | async-done | bytes 2097168 | tf_op jit(solution)/shard_map/reduce_scatter | solution.py:82
  2486.7 3.9 multiply_reduce_fusion
  2492.0 3.2 pad_maximum_fusion.1
  2495.2 39.1 %psum.98 = f32[]{:T(128)} all-reduce(f32[]{:T(128)S(6)} %add.301), channel_id=1, replica_groups=mesh['fsdp'=2,'ctx'=4,'tp'=4] {'fsdp','ctx','tp'}, use_global_device_ids=true, to_apply=%region_41.42 | all-reduce | flops 1 | bytes 8 | tf_op jit(solution)/shard_map/psum | solution.py:268
  2535.0 5.4 fusion.122
  2540.4 3.2 copy.154
  2543.6 12.4 fusion.118
  2556.0 5.5 copy.155
  2561.5 7.0 fusion.116
  2573.2 5.5 copy.158
  2583.5 5.5 copy.161
  2593.8 5.3 copy.164
  (397 shorter events, 166.6 us)
Async XLA Ops:
  7.2 105.3 %all-gather.11.cloned.1.call-start = ((), (), s32[]{:S(2)}) async-start(), calls=%async_computation.12 | async-start | bytes 7077888 | tf_op jit(solution)/shard_map/all_gather | solution.py:67
  9.6 4.2 copy-start.8
  9.7 144.5 %all-gather.21.cloned.1.call-start = ((), (), s32[]{:S(2)}) async-start(), calls=%async_computation.17 | async-start | bytes 1310720 | tf_op jit(solution)/shard_map/all_gather | solution.py:126
  14.2 118.6 %copy-start.73 = (f32[256]{0:T(256)}, f32[256]{0:T(256)S(1)}, u32[]{:S(2)}) copy-start(f32[256]{0:T(256)S(1)} %broadcast_multiply_fusion.13) | copy-start | bytes 3076
  14.2 103.0 %copy-start.75 = (f32[256]{0:T(256)}, f32[256]{0:T(256)S(1)}, u32[]{:S(2)}) copy-start(f32[256]{0:T(256)S(1)} %broadcast_multiply_fusion.11) | copy-start | bytes 3076
  14.9 102.3 %copy-start.96 = (f32[256]{0:T(256)}, f32[256]{0:T(256)S(1)}, u32[]{:S(2)}) copy-start(f32[256]{0:T(256)S(1)} %get-tuple-element.74) | copy-start | bytes 3076
  14.9 116.0 %copy-start.98 = (f32[256]{0:T(256)}, f32[256]{0:T(256)S(1)}, u32[]{:S(2)}) copy-start(f32[256]{0:T(256)S(1)} %get-tuple-element.73) | copy-start | bytes 3076
  14.9 102.2 %copy-start.88 = (f32[256]{0:T(256)}, f32[256]{0:T(256)S(1)}, u32[]{:S(2)}) copy-start(f32[256]{0:T(256)S(1)} %fusion.98) | copy-start | bytes 3076
  127.9 55.9 %all-gather.25.cloned.1.call-start = ((), (), s32[]{:S(2)}) async-start(), calls=%async_computation.31 | async-start | bytes 1310720 | tf_op jit(solution)/shard_map/all_gather | solution.py:127
  130.9 6.7 copy-start.90
  132.7 80.5 %all-gather.13.cloned.1.call-start = ((), (), s32[]{:S(2)}) async-start(), calls=%async_computation.13 | async-start | bytes 1310720 | tf_op jit(solution)/shard_map/all_gather | solution.py:126
  141.2 3.8 copy-start.51
  142.2 4.1 copy-start.103
  142.2 4.1 copy-start.106
  142.2 5.1 copy-start.101
  142.2 5.1 copy-start.105
  144.2 98.5 %all-gather.23.cloned.1.call-start = ((), (), s32[]{:S(2)}) async-start(), calls=%async_computation.30 | async-start | bytes 1310720 | tf_op jit(solution)/shard_map/all_gather | solution.py:127
  145.0 149.0 %all-gather.15.cloned.1.call-start = ((), (), s32[]{:S(2)}) async-start(), calls=%async_computation.14 | async-start | bytes 2359296 | tf_op jit(solution)/shard_map/all_gather | solution.py:71
  145.8 238.4 %all-reduce.25.cloned.1.call-start = ((), (), s32[]{:S(2)}) async-start(), calls=%async_computation.34 | async-start | bytes 8388608 | tf_op jit(solution)/shard_map/psum | solution.py:62
  185.1 65.4 %copy-start.41 = (bf16[1024,4,128]{2,1,0:T(4,128)(2,1)}, bf16[1024,4,128]{2,1,0:T(4,128)(2,1)S(1)}, u32[]{:S(2)}) copy-start(bf16[1024,4,128]{2,1,0:T(4,128)(2,1)S(1)} %reshape.480) | copy-start | bytes 3145732
  214.7 33.2 %copy-start.20 = (bf16[1024,512]{0,1:T(8,128)(2,1)}, bf16[1024,512]{0,1:T(8,128)(2,1)S(1)}, u32[]{:S(2)}) copy-start(bf16[1024,512]{0,1:T(8,128)(2,1)S(1)} %copy.185) | copy-start | bytes 3145732
  252.1 41.9 %copy-start.65 = (bf16[4,128,256]{2,1,0:T(8,128)(2,1)}, bf16[4,128,256]{2,1,0:T(8,128)(2,1)S(1)}, u32[]{:S(2)}) copy-start(bf16[4,128,256]{2,1,0:T(8,128)(2,1)S(1)} %fusion.47) | copy-start | bytes 786436
  253.3 44.5 %copy-start.63 = (bf16[4,128,256]{2,1,0:T(8,128)(2,1)}, bf16[4,128,256]{2,1,0:T(8,128)(2,1)S(1)}, u32[]{:S(2)}) copy-start(bf16[4,128,256]{2,1,0:T(8,128)(2,1)S(1)} %fusion.48) | copy-start | bytes 786436
  294.0 3.8 copy-start.27
  299.9 315.0 %all-gather.17.cloned.1.call-start = ((), (), s32[]{:S(2)}) async-start(), calls=%async_computation.15 | async-start | bytes 18874368 | tf_op jit(solution)/shard_map/all_gather | solution.py:68
  303.9 437.2 %all-gather.19.cloned.1.call-start = ((), (), s32[]{:S(2)}) async-start(), calls=%async_computation.16 | async-start | bytes 9437184 | tf_op jit(solution)/shard_map/all_gather | solution.py:72
  306.8 562.1 %all-reduce.23.cloned.1.call-start = ((), (), s32[]{:S(2)}) async-start(), calls=%async_computation.33 | async-start | bytes 8388608 | tf_op jit(solution)/shard_map/psum | solution.py:62
  389.5 238.6 %copy-start.77 = (f32[256]{0:T(256)}, f32[256]{0:T(256)S(1)}, u32[]{:S(2)}) copy-start(f32[256]{0:T(256)S(1)} %fusion.97) | copy-start | bytes 3076
  615.0 13.2 copy-start.7
  741.0 10.6 copy-start.18
  741.0 10.6 copy-start.29
  741.0 10.6 copy-start.108
  784.9 165.8 %reduce-scatter.13.cloned.1.call-start = ((), (), s32[]{:S(2)}) async-start(), calls=%async_computation.18 | async-start | bytes 2621440 | tf_op jit(solution)/shard_map/reduce_scatter | solution.py:201
  881.9 4.1 copy-start.6
  889.0 89.6 %reduce-scatter.17.cloned.1.call-start = ((), (), s32[]{:S(2)}) async-start(), calls=%async_computation.20 | async-start | bytes 2621440 | tf_op jit(solution)/shard_map/reduce_scatter | solution.py:201
  894.9 4.2 copy-start.4
  902.2 122.5 %reduce-scatter.15.cloned.1.call-start = ((), (), s32[]{:S(2)}) async-start(), calls=%async_computation.19 | async-start | bytes 2621440 | tf_op jit(solution)/shard_map/reduce_scatter | solution.py:204
  910.4 160.3 %reduce-scatter.19.cloned.1.call-start = ((), (), s32[]{:S(2)}) async-start(), calls=%async_computation.21 | async-start | bytes 2621440 | tf_op jit(solution)/shard_map/reduce_scatter | solution.py:204
  918.7 256.4 %reduce-scatter.27.cloned.1.call-start = ((), (), s32[]{:S(2)}) async-start(), calls=%async_computation.25 | async-start | bytes 2359296 | tf_op jit(solution)/shard_map/reduce_scatter | solution.py:87
  923.0 288.6 %reduce-scatter.25.cloned.1.call-start = ((), (), s32[]{:S(2)}) async-start(), calls=%async_computation.24 | async-start | bytes 2359296 | tf_op jit(solution)/shard_map/reduce_scatter | solution.py:87
  923.0 8.6 copy-start.19
  931.6 7.3 copy-start.39
  931.6 7.3 copy-start.64
  944.8 424.0 %all-reduce.21.cloned.1.call-start = ((), (), s32[]{:S(2)}) async-start(), calls=%async_computation.32 | async-start | bytes 16777216 | tf_op jit(solution)/shard_map/psum | solution.py:62
  951.3 27.3 %copy-start.60 = (f32[256,128]{0,1:T(8,128)S(1)}, f32[256,128]{0,1:T(8,128)}, u32[]{:S(2)}) copy-start(f32[256,128]{0,1:T(8,128)} %get-tuple-element.156) | copy-start | bytes 393220
  979.8 92.1 %copy-start.70 = (bf16[1,256,512]{2,1,0:T(8,128)(2,1)S(1)}, bf16[1,256,512]{2,1,0:T(8,128)(2,1)}, u32[]{:S(2)}) copy-start(bf16[1,256,512]{2,1,0:T(8,128)(2,1)} %copy.130) | copy-start | bytes 786436
  1083.9 438.0 %reduce-scatter.35.cloned.1.call-start = ((), (), s32[]{:S(2)}) async-start(), calls=%async_computation.29 | async-start | bytes 9437184 | tf_op jit(solution)/shard_map/reduce_scatter | solution.py:90
  1092.6 581.7 %reduce-scatter.33.cloned.1.call-start = ((), (), s32[]{:S(2)}) async-start(), calls=%async_computation.28 | async-start | bytes 9437184 | tf_op jit(solution)/shard_map/reduce_scatter | solution.py:90
  1101.2 694.0 %reduce-scatter.23.cloned.1.call-start = ((), (), s32[]{:S(2)}) async-start(), calls=%async_computation.23 | async-start | bytes 7077888 | tf_op jit(solution)/shard_map/reduce_scatter | solution.py:79
  1107.7 808.8 %reduce-scatter.21.cloned.1.call-start = ((), (), s32[]{:S(2)}) async-start(), calls=%async_computation.22 | async-start | bytes 7077888 | tf_op jit(solution)/shard_map/reduce_scatter | solution.py:79
  1114.5 1086.9 %reduce-scatter.31.cloned.1.call-start = ((), (), s32[]{:S(2)}) async-start(), calls=%async_computation.27 | async-start | bytes 18874368 | tf_op jit(solution)/shard_map/reduce_scatter | solution.py:82
  1129.2 1357.5 %reduce-scatter.29.cloned.1.call-start = ((), (), s32[]{:S(2)}) async-start(), calls=%async_computation.26 | async-start | bytes 18874368 | tf_op jit(solution)/shard_map/reduce_scatter | solution.py:82
  1368.8 3.7 copy-start.97
  1368.8 3.8 copy-start.9
  1368.8 4.1 copy-start.16
  1368.8 4.7 copy-start.17
  1378.2 3.9 copy-start.55
  2491.9 43.0 %copy-start.34 = (f32[3,256,512]{1,2,0:T(8,128)S(1)}, f32[3,256,512]{1,2,0:T(8,128)}, u32[]{:S(2)}) copy-start(f32[3,256,512]{1,2,0:T(8,128)} %copy.149) | copy-start | bytes 4718596
  2492.0 43.0 %copy-start.35 = (f32[3,256,512]{1,2,0:T(8,128)S(1)}, f32[3,256,512]{1,2,0:T(8,128)}, u32[]{:S(2)}) copy-start(f32[3,256,512]{1,2,0:T(8,128)} %copy.145) | copy-start | bytes 4718596
  2556.0 5.5 copy-start.22
  2556.0 5.5 copy-start.37
  2573.2 5.5 copy-start.25
  2583.5 5.5 copy-start.24
  2599.2 4.2 copy-start.23
  (68 other events, 128.7 us)
Sparse Core Ops, SparseCore 0:
  10.8 101.7 all-gather.10
  128.0 26.1 all-gather.20
  156.3 27.4 all-gather.24
  185.8 27.4 all-gather.12
  215.2 27.4 all-gather.22
  245.2 48.7 all-gather.14
  300.1 84.1 all-reduce.24
  387.2 227.7 all-gather.16
  617.9 123.0 all-gather.18
  785.1 83.8 all-reduce.22
  889.1 43.9 reduce-scatter.12
  935.4 43.1 reduce-scatter.16
  981.5 43.1 reduce-scatter.14
  1027.5 43.1 reduce-scatter.18
  1074.1 67.0 reduce-scatter.26
  1144.6 66.9 reduce-scatter.24
  1215.8 152.9 all-reduce.20
  1372.3 149.5 reduce-scatter.34
  1525.9 148.4 reduce-scatter.32
  1677.8 117.3 reduce-scatter.22
  1798.8 117.5 reduce-scatter.20
  1920.2 281.0 reduce-scatter.30
  2205.6 281.0 reduce-scatter.28
where the time goes:
time: 2630 us; the launch traced here: 2620 us
  waiting for transfers between devices  2120 us (81%)
  matrix products  204 us (8%)
  local copies, waits for them, and re-layouts  129 us (5%)
  other arithmetic  101 us (4%)
  blocking collectives  39.1 us (1%)
    reduce_scatter x2, waiting for transfers between devices, reduce_grads(): lax.psum_scatter(proj_grad.astype(jnp.bfloat16), ('fsdp', 'ctx'), scatter...  567 us
    psum x3, waiting for transfers between devices, tensor_sum(): return lax.psum(partial_sum, 'tp')  315 us
    reduce_scatter x2, waiting for transfers between devices, reduce_grads(): lax.psum_scatter(down_grad.astype(jnp.bfloat16), ('fsdp', 'ctx'), scatter...  289 us
    reduce_scatter x2, waiting for transfers between devices, reduce_grads(): lax.psum_scatter(att_grad.astype(jnp.bfloat16), ('fsdp', 'ctx'), scatter_...  239 us
    all_gather x1, waiting for transfers between devices, gather_weights(): lax.all_gather(ff_proj.astype(jnp.bfloat16), ('fsdp', 'ctx'), axis=1, til...  225 us
    all_gather x1, waiting for transfers between devices, gather_weights(): lax.all_gather(ff_out.astype(jnp.bfloat16), ('fsdp', 'ctx'), axis=0, tile...  107 us
    unnamed x242, local copies, waits for them, and re-layouts  102 us
    all_gather x1, waiting for transfers between devices, gather_weights(): lax.all_gather(att_proj.astype(jnp.bfloat16), ('fsdp', 'ctx'), axis=1, ti...  97.6 us
  transfers between devices with their start and end apart: 23, of which 21 were waited for; matrix products, arithmetic and copies ran while one was open for 10% of the time, Pallas kernels for 0%

commit v1 on v0

--- a/solution.py
+++ b/solution.py
@@ -59,7 +59,7 @@
 
 
 def tensor_sum(partial_sum):
-    return lax.psum(partial_sum, "tp")
+    return jnp.sum(lax.all_gather(partial_sum, "tp"), axis=0)
 
 
 def gather_weights(att_proj, attn_out, ff_proj, ff_out):

time: 2630 us -> 2750 us (1.046)
  waiting for transfers between devices: 2120 us -> 2190 us
  other arithmetic: 101 us -> 161 us
    all_gather x0 -> x8, waiting for transfers between devices: none -> 328 us  [tensor_sum(): return jnp.sum(lax.all_gather(partial_sum, 'tp'), axis=0)]
    psum x3 -> x0, waiting for transfers between devices: 315 us -> none  [tensor_sum(): return lax.psum(partial_sum, 'tp')]
    reduce_scatter x2, waiting for transfers between devices: 36.4 us -> 135 us  [reduce_grads(): lax.psum_scatter(out_grad.astype(jnp.bfloat16), ('fsdp', 'ctx'), scatter_...]
    reduce_scatter x2, waiting for transfers between devices: 289 us -> 235 us  [reduce_grads(): lax.psum_scatter(down_grad.astype(jnp.bfloat16), ('fsdp', 'ctx'), scatter...]
    reduce_sum x0 -> x8, other arithmetic: none -> 45.9 us  [tensor_sum(): return jnp.sum(lax.all_gather(partial_sum, 'tp'), axis=0)]
    unnamed x242 -> x248, local copies, waits for them, and re-layouts: 102 us -> 96.1 us
  transfers between devices with their start and end apart: 23 -> 28, of which waited for: 21 -> 27; matrix products, arithmetic and copies ran while one was open for 10% -> 12% of each run, Pallas kernels for 0% -> 0%
where the time goes in v1:
time: 2750 us
  waiting for transfers between devices  2190 us (80%)
  matrix products  206 us (7%)
  other arithmetic  161 us (6%)
  local copies, waits for them, and re-layouts  123 us (4%)
  blocking collectives  39.1 us (1%)
    reduce_scatter x2, waiting for transfers between devices, reduce_grads(): lax.psum_scatter(proj_grad.astype(jnp.bfloat16), ('fsdp', 'ctx'), scatter...  566 us
    all_gather x8, waiting for transfers between devices, tensor_sum(): return jnp.sum(lax.all_gather(partial_sum, 'tp'), axis=0)  328 us
    reduce_scatter x2, waiting for transfers between devices, reduce_grads(): lax.psum_scatter(att_grad.astype(jnp.bfloat16), ('fsdp', 'ctx'), scatter_...  239 us
    reduce_scatter x2, waiting for transfers between devices, reduce_grads(): lax.psum_scatter(down_grad.astype(jnp.bfloat16), ('fsdp', 'ctx'), scatter...  235 us
    all_gather x1, waiting for transfers between devices, gather_weights(): lax.all_gather(ff_proj.astype(jnp.bfloat16), ('fsdp', 'ctx'), axis=1, til...  219 us
    reduce_scatter x2, waiting for transfers between devices, reduce_grads(): lax.psum_scatter(out_grad.astype(jnp.bfloat16), ('fsdp', 'ctx'), scatter_...  135 us
    all_gather x1, waiting for transfers between devices, gather_weights(): lax.all_gather(ff_out.astype(jnp.bfloat16), ('fsdp', 'ctx'), axis=0, tile...  115 us
    all_gather x1, waiting for transfers between devices, gather_weights(): lax.all_gather(att_proj.astype(jnp.bfloat16), ('fsdp', 'ctx'), axis=1, ti...  97.6 us
  transfers between devices with their start and end apart: 28, of which 27 were waited for; matrix products, arithmetic and copies ran while one was open for 12% of the time, Pallas kernels for 0%

profile of v1, /device:TPU:0, one launch (start us, length us, event | category | flops | bytes accessed | tf_op | source)
XLA Modules:
  0.0 2746.3 jit_solution(248620134804033783)
XLA Ops:
  14.9 97.6 %all-gather.27.cloned.1.call-done = bf16[3,2048,512]{2,1,0:T(8,128)(2,1)} async-done(((bf16[3,256,512]{2,1,0:T(8,128)(2,1)}), bf16[3,2048,512]{2,1,0:T(8,128)(2,1)}) %all-gather.27.cloned.1.call-update) | async-done | bytes 6291472 | tf_op jit(solution)/shard_map/all_gather | solution.py:67
  145.0 10.2 all-gather.29.cloned.1.call-done
  156.6 28.1 %all-gather.39.cloned.1.call-done = bf16[1,1024,512]{2,1,0:T(8,128)(2,1)} async-done(((bf16[1,256,512]{2,1,0:T(8,128)(2,1)}), bf16[1,1024,512]{2,1,0:T(8,128)(2,1)}) %all-gather.39.cloned.1.call-update) | async-done | bytes 1048592 | tf_op jit(solution)/shard_map/all_gather | solution.py:127
  190.5 45.6 %all-gather.31.cloned.1.call-done = bf16[2048,512]{1,0:T(8,128)(2,1)} async-done(((bf16[256,512]{1,0:T(8,128)(2,1)}), bf16[2048,512]{1,0:T(8,128)(2,1)}) %all-gather.31.cloned.1.call-update) | async-done | bytes 2097168 | tf_op jit(solution)/shard_map/all_gather | solution.py:71
  241.5 23.1 all-gather.37.cloned.1.call-done
  266.1 28.0 %all-gather.45.cloned.1.call-done = bf16[1,1024,512]{2,1,0:T(8,128)(2,1)} async-done(((bf16[1,256,512]{2,1,0:T(8,128)(2,1)}), bf16[1,1024,512]{2,1,0:T(8,128)(2,1)}) %all-gather.45.cloned.1.call-update) | async-done | bytes 1048592 | tf_op jit(solution)/shard_map/all_gather | solution.py:127
  311.3 42.6 %all-gather.41.cloned.1.call-done = f32[1024,2048]{1,0:T(8,128)} async-done(((f32[256,2048]{1,0:T(8,128)}), f32[1024,2048]{1,0:T(8,128)}) %all-gather.41.cloned.1.call-update) | async-done | bytes 8388624 | tf_op jit(solution)/shard_map/all_gather | solution.py:62
  354.0 5.7 reduce_sum.358
  359.7 54.7 %all-gather.47.cloned.1.call-done = f32[1024,2048]{1,0:T(8,128)} async-done(((f32[256,2048]{1,0:T(8,128)}), f32[1024,2048]{1,0:T(8,128)}) %all-gather.47.cloned.1.call-update) | async-done | bytes 8388624 | tf_op jit(solution)/shard_map/all_gather | solution.py:62
  414.4 5.7 reduce_sum.368
  420.2 5.2 fusion.146
  425.7 219.1 %all-gather.33.cloned.1.call-done = bf16[2,2048,2048]{2,1,0:T(8,128)(2,1)} async-done(((bf16[2,256,2048]{2,1,0:T(8,128)(2,1)}), bf16[2,2048,2048]{2,1,0:T(8,128)(2,1)}) %all-gather.33.cloned.1.call-update) | async-done | bytes 16777232 | tf_op jit(solution)/shard_map/all_gather | solution.py:68
  644.8 10.3 convolution_bitcast_fusion.1
  655.1 115.4 %all-gather.35.cloned.1.call-done = bf16[2048,2048]{1,0:T(8,128)(2,1)} async-done(((bf16[256,2048]{1,0:T(8,128)(2,1)}), bf16[2048,2048]{1,0:T(8,128)(2,1)}) %all-gather.35.cloned.1.call-update) | async-done | bytes 8388624 | tf_op jit(solution)/shard_map/all_gather | solution.py:72
  770.5 10.4 multiply_bitcast_fusion.3
  780.9 13.5 convolution_bitcast_fusion.5
  797.8 11.0 convolution_bitcast_fusion
  808.9 5.6 multiply_bitcast_fusion.1
  814.4 13.5 convolution_bitcast_fusion.4
  829.2 21.9 all-gather.51.cloned.1.call-done
  851.1 5.7 reduce_sum.374
  859.4 51.4 %all-gather.55.cloned.1.call-done = f32[1024,2048]{1,0:T(8,128)} async-done(((f32[256,2048]{1,0:T(8,128)}), f32[1024,2048]{1,0:T(8,128)}) %all-gather.55.cloned.1.call-update) | async-done | bytes 8388624 | tf_op jit(solution)/shard_map/all_gather | solution.py:62
  910.8 5.9 reduce_sum.383
  965.8 8.3 fusion.65
  982.7 43.1 %reduce-scatter.19.cloned.1.call-done = f32[256,512]{1,0:T(8,128)} async-done(((f32[1024,512]{1,0:T(8,128)}), f32[256,512]{1,0:T(8,128)}) %reduce-scatter.19.cloned.1.call-update) | async-done | bytes 524304 | tf_op jit(solution)/shard_map/reduce_scatter | solution.py:204
  1026.8 6.1 convolution_bitcast_fusion.2
  1036.7 34.4 %reduce-scatter.13.cloned.1.call-done = f32[256,512]{0,1:T(8,128)} async-done(((f32[1024,512]{0,1:T(8,128)}), f32[256,512]{0,1:T(8,128)}) %reduce-scatter.13.cloned.1.call-update) | async-done | bytes 524304 | tf_op jit(solution)/shard_map/reduce_scatter | solution.py:201
  1072.6 44.6 %reduce-scatter.15.cloned.1.call-done = f32[256,512]{1,0:T(8,128)} async-done(((f32[1024,512]{1,0:T(8,128)}), f32[256,512]{1,0:T(8,128)}) %reduce-scatter.15.cloned.1.call-update) | async-done | bytes 524304 | tf_op jit(solution)/shard_map/reduce_scatter | solution.py:204
  1118.2 5.9 convolution_bitcast_fusion.3
  1124.2 10.6 fusion.63
  1135.1 8.4 convert_bitcast_fusion.2
  1143.5 8.3 convert_bitcast_fusion.3
  1152.9 5.8 convert_bitcast_fusion.4
  1159.7 5.8 convert_bitcast_fusion.5
  1166.0 10.2 all-gather.49.cloned.1.call-done
  1176.2 5.7 reduce_sum.372
  1181.9 54.6 %all-gather.57.cloned.1.call-done = f32[1024,2048]{1,0:T(8,128)} async-done(((f32[256,2048]{1,0:T(8,128)}), f32[1024,2048]{1,0:T(8,128)}) %all-gather.57.cloned.1.call-update) | async-done | bytes 8388624 | tf_op jit(solution)/shard_map/all_gather | solution.py:62
  1236.5 5.7 reduce_sum.387
  1242.2 54.7 %all-gather.53.cloned.1.call-done = f32[1024,2048]{1,0:T(8,128)} async-done(((f32[256,2048]{1,0:T(8,128)}), f32[1024,2048]{1,0:T(8,128)}) %all-gather.53.cloned.1.call-update) | async-done | bytes 8388624 | tf_op jit(solution)/shard_map/all_gather | solution.py:62
  1297.0 5.7 reduce_sum.378
  1318.8 37.9 %all-gather.43.cloned.1.call-done = f32[1024,2048]{1,0:T(8,128)} async-done(((f32[256,2048]{1,0:T(8,128)}), f32[1024,2048]{1,0:T(8,128)}) %all-gather.43.cloned.1.call-update) | async-done | bytes 8388624 | tf_op jit(solution)/shard_map/all_gather | solution.py:62
  1356.7 5.7 reduce_sum.362
  1362.4 6.1 fusion.26
  1370.9 14.0 convert_bitcast_fusion
  1385.0 11.4 convert_bitcast_fusion.1
  1399.5 5.7 copy.151
  1411.7 5.4 copy.146
  1417.1 5.6 copy.143
  1427.4 82.4 %reduce-scatter.35.cloned.1.call-done = bf16[256,2048]{0,1:T(8,128)(2,1)} async-done(((bf16[2048,2048]{0,1:T(8,128)(2,1)}), bf16[256,2048]{0,1:T(8,128)(2,1)}) %reduce-scatter.35.cloned.1.call-update) | async-done | bytes 1048592 | tf_op jit(solution)/shard_map/reduce_scatter | solution.py:90
  1509.8 152.6 %reduce-scatter.33.cloned.1.call-done = bf16[256,2048]{0,1:T(8,128)(2,1)} async-done(((bf16[2048,2048]{0,1:T(8,128)(2,1)}), bf16[256,2048]{0,1:T(8,128)(2,1)}) %reduce-scatter.33.cloned.1.call-update) | async-done | bytes 1048592 | tf_op jit(solution)/shard_map/reduce_scatter | solution.py:90
  1665.0 118.3 %reduce-scatter.23.cloned.1.call-done = bf16[3,256,512]{1,2,0:T(8,128)(2,1)} async-done(((bf16[3,2048,512]{1,2,0:T(8,128)(2,1)}), bf16[3,256,512]{1,2,0:T(8,128)(2,1)}) %reduce-scatter.23.cloned.1.call-update) | async-done | bytes 786448 | tf_op jit(solution)/shard_map/reduce_scatter | solution.py:79
  1783.3 121.0 %reduce-scatter.21.cloned.1.call-done = bf16[3,256,512]{1,2,0:T(8,128)(2,1)} async-done(((bf16[3,2048,512]{1,2,0:T(8,128)(2,1)}), bf16[3,256,512]{1,2,0:T(8,128)(2,1)}) %reduce-scatter.21.cloned.1.call-update) | async-done | bytes 786448 | tf_op jit(solution)/shard_map/reduce_scatter | solution.py:79
  1910.8 64.7 %reduce-scatter.27.cloned.1.call-done = bf16[256,512]{1,0:T(8,128)(2,1)} async-done(((bf16[2048,512]{1,0:T(8,128)(2,1)}), bf16[256,512]{1,0:T(8,128)(2,1)}) %reduce-scatter.27.cloned.1.call-update) | async-done | bytes 262160 | tf_op jit(solution)/shard_map/reduce_scatter | solution.py:87
  1975.4 70.3 %reduce-scatter.25.cloned.1.call-done = bf16[256,512]{1,0:T(8,128)(2,1)} async-done(((bf16[2048,512]{1,0:T(8,128)(2,1)}), bf16[256,512]{1,0:T(8,128)(2,1)}) %reduce-scatter.25.cloned.1.call-update) | async-done | bytes 262160 | tf_op jit(solution)/shard_map/reduce_scatter | solution.py:87
  2049.5 280.9 %reduce-scatter.31.cloned.1.call-done = bf16[2,256,2048]{1,2,0:T(8,128)(2,1)} async-done(((bf16[2,2048,2048]{1,2,0:T(8,128)(2,1)}), bf16[2,256,2048]{1,2,0:T(8,128)(2,1)}) %reduce-scatter.31.cloned.1.call-update) | async-done | bytes 2097168 | tf_op jit(solution)/shard_map/reduce_scatter | solution.py:82
  2330.4 285.3 %reduce-scatter.29.cloned.1.call-done = bf16[2,256,2048]{1,2,0:T(8,128)(2,1)} async-done(((bf16[2,2048,2048]{1,2,0:T(8,128)(2,1)}), bf16[2,256,2048]{1,2,0:T(8,128)(2,1)}) %reduce-scatter.29.cloned.1.call-update) | async-done | bytes 2097168 | tf_op jit(solution)/shard_map/reduce_scatter | solution.py:82
  2624.1 39.1 %psum.34 = f32[]{:T(128)} all-reduce(f32[]{:T(128)S(6)} %add.311), channel_id=1, replica_groups=mesh['fsdp'=2,'ctx'=4,'tp'=4] {'fsdp','ctx','tp'}, use_global_device_ids=true, to_apply=%region_41.42 | all-reduce | flops 1 | bytes 8 | tf_op jit(solution)/shard_map/psum | solution.py:268
  2663.9 5.4 fusion.140
  2672.6 12.4 fusion.136
  2685.0 5.5 copy.155
  2690.5 7.0 fusion.134
  2702.1 5.5 copy.158
  2712.5 5.5 copy.161
  2722.8 5.3 copy.164
  (425 shorter events, 224.7 us)
Async XLA Ops:
  7.2 105.3 %all-gather.27.cloned.1.call-start = ((), (), s32[]{:S(2)}) async-start(), calls=%async_computation.12 | async-start | bytes 7077888 | tf_op jit(solution)/shard_map/all_gather | solution.py:67
  9.7 145.5 %all-gather.29.cloned.1.call-start = ((), (), s32[]{:S(2)}) async-start(), calls=%async_computation.13 | async-start | bytes 1310720 | tf_op jit(solution)/shard_map/all_gather | solution.py:126
  13.6 109.2 %copy-start.50 = (f32[256,128]{0,1:T(8,128)}, f32[256,128]{0,1:T(8,128)S(1)}, u32[]{:S(2)}) copy-start(f32[256,128]{0,1:T(8,128)S(1)} %get-tuple-element.151) | copy-start | bytes 393220
  14.2 103.0 %copy-start.78 = (f32[256]{0:T(256)}, f32[256]{0:T(256)S(1)}, u32[]{:S(2)}) copy-start(f32[256]{0:T(256)S(1)} %broadcast_multiply_fusion.13) | copy-start | bytes 3076
  14.2 118.9 %copy-start.80 = (f32[256]{0:T(256)}, f32[256]{0:T(256)S(1)}, u32[]{:S(2)}) copy-start(f32[256]{0:T(256)S(1)} %broadcast_multiply_fusion.11) | copy-start | bytes 3076
  14.9 102.3 %copy-start.93 = (f32[256]{0:T(256)}, f32[256]{0:T(256)S(1)}, u32[]{:S(2)}) copy-start(f32[256]{0:T(256)S(1)} %get-tuple-element.73) | copy-start | bytes 3076
  14.9 118.2 %copy-start.91 = (f32[256]{0:T(256)}, f32[256]{0:T(256)S(1)}, u32[]{:S(2)}) copy-start(f32[256]{0:T(256)S(1)} %get-tuple-element.74) | copy-start | bytes 3076
  14.9 102.3 %copy-start.87 = (f32[256]{0:T(256)}, f32[256]{0:T(256)S(1)}, u32[]{:S(2)}) copy-start(f32[256]{0:T(256)S(1)} %fusion.116) | copy-start | bytes 3076
  124.7 6.0 copy-start.44
  128.9 55.9 %all-gather.39.cloned.1.call-start = ((), (), s32[]{:S(2)}) async-start(), calls=%async_computation.30 | async-start | bytes 1310720 | tf_op jit(solution)/shard_map/all_gather | solution.py:127
  130.7 105.4 %all-gather.31.cloned.1.call-start = ((), (), s32[]{:S(2)}) async-start(), calls=%async_computation.14 | async-start | bytes 2359296 | tf_op jit(solution)/shard_map/all_gather | solution.py:71
  131.6 133.0 %all-gather.37.cloned.1.call-start = ((), (), s32[]{:S(2)}) async-start(), calls=%async_computation.17 | async-start | bytes 1310720 | tf_op jit(solution)/shard_map/all_gather | solution.py:126
  142.6 151.4 %all-gather.45.cloned.1.call-start = ((), (), s32[]{:S(2)}) async-start(), calls=%async_computation.33 | async-start | bytes 1310720 | tf_op jit(solution)/shard_map/all_gather | solution.py:127
  144.5 41.7 %copy-start.55 = (pred[256,1024]{1,0:T(8,128)(4,1)S(1)}, pred[256,1024]{1,0:T(8,128)(4,1)}, u32[]{:S(2)}) copy-start(pred[256,1024]{1,0:T(8,128)(4,1)} %compare_and_fusion.1) | copy-start | bytes 786436
  144.5 209.5 %all-gather.41.cloned.1.call-start = ((), (), s32[]{:S(2)}) async-start(), calls=%async_computation.31 | async-start | bytes 10485760 | tf_op jit(solution)/shard_map/all_gather | solution.py:62
  190.5 49.3 %copy-start.56 = (bf16[4,128,256]{2,1,0:T(8,128)(2,1)}, bf16[4,128,256]{2,1,0:T(8,128)(2,1)S(1)}, u32[]{:S(2)}) copy-start(bf16[4,128,256]{2,1,0:T(8,128)(2,1)S(1)} %fusion.60) | copy-start | bytes 786436
  239.8 174.6 %all-gather.47.cloned.1.call-start = ((), (), s32[]{:S(2)}) async-start(), calls=%async_computation.34 | async-start | bytes 10485760 | tf_op jit(solution)/shard_map/all_gather | solution.py:62
  266.1 31.8 %copy-start.16 = (bf16[1024,512]{0,1:T(8,128)(2,1)}, bf16[1024,512]{0,1:T(8,128)(2,1)S(1)}, u32[]{:S(2)}) copy-start(bf16[1024,512]{0,1:T(8,128)(2,1)S(1)} %copy.186) | copy-start | bytes 3145732
  304.0 340.8 %all-gather.33.cloned.1.call-start = ((), (), s32[]{:S(2)}) async-start(), calls=%async_computation.15 | async-start | bytes 18874368 | tf_op jit(solution)/shard_map/all_gather | solution.py:68
  308.4 462.1 %all-gather.35.cloned.1.call-start = ((), (), s32[]{:S(2)}) async-start(), calls=%async_computation.16 | async-start | bytes 9437184 | tf_op jit(solution)/shard_map/all_gather | solution.py:72
  311.1 540.0 %all-gather.51.cloned.1.call-start = ((), (), s32[]{:S(2)}) async-start(), calls=%async_computation.36 | async-start | bytes 10485760 | tf_op jit(solution)/shard_map/all_gather | solution.py:62
  425.7 229.4 %copy-start.84 = (f32[256]{0:T(256)}, f32[256]{0:T(256)S(1)}, u32[]{:S(2)}) copy-start(f32[256]{0:T(256)S(1)} %multiply_reduce_fusion.7) | copy-start | bytes 3076
  425.7 229.4 %copy-start.72 = (f32[256]{0:T(256)}, f32[256]{0:T(256)S(1)}, u32[]{:S(2)}) copy-start(f32[256]{0:T(256)S(1)} %fusion.117) | copy-start | bytes 3076
  794.4 116.4 %all-gather.55.cloned.1.call-start = ((), (), s32[]{:S(2)}) async-start(), calls=%async_computation.38 | async-start | bytes 10485760 | tf_op jit(solution)/shard_map/all_gather | solution.py:62
  795.1 13.7 slice-start
  797.8 11.0 copy-start.75
  797.8 11.0 copy-start.42
  797.8 11.0 slice-start.1
  808.9 5.6 copy-start.15
  828.0 152.5 %reduce-scatter.17.cloned.1.call-start = ((), (), s32[]{:S(2)}) async-start(), calls=%async_computation.20 | async-start | bytes 2621440 | tf_op jit(solution)/shard_map/reduce_scatter | solution.py:201
  920.2 5.1 copy-start.25
  920.2 5.1 copy-start.43
  935.7 90.0 %reduce-scatter.19.cloned.1.call-start = ((), (), s32[]{:S(2)}) async-start(), calls=%async_computation.21 | async-start | bytes 2621440 | tf_op jit(solution)/shard_map/reduce_scatter | solution.py:204
  943.2 127.9 %reduce-scatter.13.cloned.1.call-start = ((), (), s32[]{:S(2)}) async-start(), calls=%async_computation.18 | async-start | bytes 2621440 | tf_op jit(solution)/shard_map/reduce_scatter | solution.py:201
  957.5 159.6 %reduce-scatter.15.cloned.1.call-start = ((), (), s32[]{:S(2)}) async-start(), calls=%async_computation.19 | async-start | bytes 2621440 | tf_op jit(solution)/shard_map/reduce_scatter | solution.py:204
  965.8 210.4 %all-gather.49.cloned.1.call-start = ((), (), s32[]{:S(2)}) async-start(), calls=%async_computation.35 | async-start | bytes 10485760 | tf_op jit(solution)/shard_map/all_gather | solution.py:62
  974.2 262.3 %all-gather.57.cloned.1.call-start = ((), (), s32[]{:S(2)}) async-start(), calls=%async_computation.39 | async-start | bytes 10485760 | tf_op jit(solution)/shard_map/all_gather | solution.py:62
  1033.0 264.0 %all-gather.53.cloned.1.call-start = ((), (), s32[]{:S(2)}) async-start(), calls=%async_computation.37 | async-start | bytes 10485760 | tf_op jit(solution)/shard_map/all_gather | solution.py:62
  1036.4 34.7 %copy-start.53 = (f32[256,128]{0,1:T(8,128)S(1)}, f32[256,128]{0,1:T(8,128)}, u32[]{:S(2)}) copy-start(f32[256,128]{0,1:T(8,128)} %get-tuple-element.150) | copy-start | bytes 393220
  1036.4 35.9 %copy-start.51 = (f32[256,128]{0,1:T(8,128)S(1)}, f32[256,128]{0,1:T(8,128)}, u32[]{:S(2)}) copy-start(f32[256,128]{0,1:T(8,128)} %copy-done.50) | copy-start | bytes 393220
  1072.6 51.6 %copy-start.69 = (bf16[1,256,512]{2,1,0:T(8,128)(2,1)}, bf16[1,256,512]{2,1,0:T(8,128)(2,1)S(1)}, u32[]{:S(2)}) copy-start(bf16[1,256,512]{2,1,0:T(8,128)(2,1)S(1)} %copy.179) | copy-start | bytes 786436
  1124.2 232.5 %all-gather.43.cloned.1.call-start = ((), (), s32[]{:S(2)}) async-start(), calls=%async_computation.32 | async-start | bytes 10485760 | tf_op jit(solution)/shard_map/all_gather | solution.py:62
  1134.9 374.9 %reduce-scatter.35.cloned.1.call-start = ((), (), s32[]{:S(2)}) async-start(), calls=%async_computation.29 | async-start | bytes 9437184 | tf_op jit(solution)/shard_map/reduce_scatter | solution.py:90
  1143.5 518.8 %reduce-scatter.33.cloned.1.call-start = ((), (), s32[]{:S(2)}) async-start(), calls=%async_computation.28 | async-start | bytes 9437184 | tf_op jit(solution)/shard_map/reduce_scatter | solution.py:90
  1151.9 631.4 %reduce-scatter.23.cloned.1.call-start = ((), (), s32[]{:S(2)}) async-start(), calls=%async_computation.23 | async-start | bytes 7077888 | tf_op jit(solution)/shard_map/reduce_scatter | solution.py:79
  1158.8 745.6 %reduce-scatter.21.cloned.1.call-start = ((), (), s32[]{:S(2)}) async-start(), calls=%async_computation.22 | async-start | bytes 7077888 | tf_op jit(solution)/shard_map/reduce_scatter | solution.py:79
  1165.6 809.9 %reduce-scatter.27.cloned.1.call-start = ((), (), s32[]{:S(2)}) async-start(), calls=%async_computation.25 | async-start | bytes 2359296 | tf_op jit(solution)/shard_map/reduce_scatter | solution.py:87
  1302.7 5.3 copy-start.8
  1302.7 6.2 copy-start.9
  1318.8 726.9 %reduce-scatter.25.cloned.1.call-start = ((), (), s32[]{:S(2)}) async-start(), calls=%async_computation.24 | async-start | bytes 2359296 | tf_op jit(solution)/shard_map/reduce_scatter | solution.py:87
  1356.7 5.7 copy-start.74
  1356.7 5.7 copy-start.100
  1362.4 6.1 copy-start.57
  1370.7 959.7 %reduce-scatter.31.cloned.1.call-start = ((), (), s32[]{:S(2)}) async-start(), calls=%async_computation.27 | async-start | bytes 18874368 | tf_op jit(solution)/shard_map/reduce_scatter | solution.py:82
  1385.0 1230.7 %reduce-scatter.29.cloned.1.call-start = ((), (), s32[]{:S(2)}) async-start(), calls=%async_computation.26 | async-start | bytes 18874368 | tf_op jit(solution)/shard_map/reduce_scatter | solution.py:82
  1399.5 5.7 copy-start.23
  1417.1 5.6 copy-start.47
  1427.4 479.4 %copy-start.26 = (f32[1,256,2048]{2,1,0:T(8,128)S(1)}, f32[1,256,2048]{2,1,0:T(8,128)}, u32[]{:S(2)}) copy-start(f32[1,256,2048]{2,1,0:T(8,128)} %get-tuple-element.97) | copy-start | bytes 6291460
  2620.9 43.0 %copy-start.29 = (f32[3,256,512]{1,2,0:T(8,128)S(1)}, f32[3,256,512]{1,2,0:T(8,128)}, u32[]{:S(2)}) copy-start(f32[3,256,512]{1,2,0:T(8,128)} %copy.149) | copy-start | bytes 4718596
  2620.9 43.0 %copy-start.30 = (f32[3,256,512]{1,2,0:T(8,128)S(1)}, f32[3,256,512]{1,2,0:T(8,128)}, u32[]{:S(2)}) copy-start(f32[3,256,512]{1,2,0:T(8,128)} %copy.145) | copy-start | bytes 4718596
  2685.0 5.5 copy-start.18
  2685.0 5.5 copy-start.32
  2702.1 5.5 copy-start.21
  2712.5 5.5 copy-start.20
  (76 other events, 171.9 us)
Sparse Core Ops, SparseCore 0:
  10.8 101.7 all-gather.26
  129.0 26.1 all-gather.28
  157.3 27.4 all-gather.38
  187.3 48.7 all-gather.30
  238.1 26.4 all-gather.36
  266.6 27.4 all-gather.44
  296.2 57.7 all-gather.40
  356.1 58.2 all-gather.46
  417.2 227.5 all-gather.32
  647.3 123.0 all-gather.34
  794.6 56.4 all-gather.50
  852.5 58.2 all-gather.54
  935.8 43.8 reduce-scatter.16
  982.6 43.1 reduce-scatter.18
  1027.9 43.1 reduce-scatter.12
  1073.9 43.1 reduce-scatter.14
  1118.6 57.6 all-gather.48
  1178.2 58.2 all-gather.56
  1238.6 58.2 all-gather.52
  1298.4 58.2 all-gather.42
  1360.3 149.3 reduce-scatter.34
  1513.8 148.4 reduce-scatter.32
  1665.9 117.3 reduce-scatter.22
  1786.8 117.5 reduce-scatter.20
  1908.5 66.8 reduce-scatter.26
  1978.8 66.8 reduce-scatter.24
  2049.3 281.0 reduce-scatter.30
  2334.6 281.0 reduce-scatter.28
